TPU v7x, 256 devices: a whole 4x4x8 slice. The times are simulated.
256 devices in a mesh: expert: 16 (over y, x), tensor: 16 (over z, core).
Axes of the slice: x: 4, y: 4, z: 8, core: 2. Of those that a mesh axis runs over, the one named last changes fastest.
Arguments:
- queries: bfloat16 [4096, 8192], P('expert', 'tensor'), may hold values from -8 to 8
- keys_values: bfloat16 [16, 4, 1280, 256], P('expert'), may hold values from -6 to 6
- prefix_len: int32 [16], P('expert'), may hold values from 128 to 1024, as said below
- out_proj: bfloat16 [8192, 4096], P('tensor', 'expert'), may hold values from -0.0625 to 0.0625
- residual: bfloat16 [4096, 4096], P(('expert', 'tensor')), may hold values from -1.796875 to 1.796875
- norm_gain: float32 [4096], replicated, may hold values from 0.1 to 1.9
- expert_ids: int32 [4096, 8], P('expert'), may hold values from 0 to 63, all different within a row; in each aligned block of 16 rows (0 to 15, 16 to 31, ...) at most 3 rows name the same one
- route_weights: bfloat16 [4096, 8], P('expert'), may hold values from 0.19921875 to 1
- w_gate: bfloat16 [256, 4096, 384], P(('expert', 'tensor')), may hold values from -0.09375 to 0.09375
- w_up: bfloat16 [256, 4096, 384], P(('expert', 'tensor')), may hold values from -0.09375 to 0.09375
- w_down: bfloat16 [256, 384, 4096], P(('expert', 'tensor')), may hold values from -0.15625 to 0.15625
Outputs:
- layer_out: bfloat16 [4096, 4096], P(('expert', 'tensor'))
Inputs may be any that keep to these rules, and one draw needn't show every extreme that they name: `expert_ids`: in the rows of one device (aligned blocks of 16 rows) no expert is named by more than 3 rows, a bound that some block reaches; a row names 8 different experts. `prefix_len`: some sequence has all 1024 slots live.
All inputs are finite; a program needn't handle non-finite values.
Results may differ from a plain program's by a relative error of at most 0.035.
Values may be sent and summed in bfloat16 or wider, within the bound.
No kernel may reach another device: no remote copies, remote signals or barrier semaphores. Data moves between devices by JAX's collectives and lax.ppermute only.
A program may use at most 128 MiB of HBM per device.

v0:
```python
import math
import jax
import jax.numpy as jnp
from jax import lax
from jax.sharding import PartitionSpec as P

HEADS = 64
KVH = 4
HD = 128
TOPK = 8
HSPLIT = 4
TOK_DEV = 16
PREFIX = 1024


def norm_rows(hidden_state, norm_gain):
    values = hidden_state.astype(jnp.float32)
    factor = lax.rsqrt(jnp.mean(values * values, axis=-1, keepdims=True) + 1e-06)
    return (values * factor * norm_gain[None, :]).astype(jnp.bfloat16)


def route_tables(expert_ids, route_weights, experts, most_rows):
    total_rows = expert_ids.shape[0]
    named_mask = expert_ids[:, :, None] == jnp.arange(experts, dtype=jnp.int32)[None, None, :]
    hit_table = jnp.sum(named_mask.astype(jnp.int32), axis=1)
    weight_table = jnp.sum(
        jnp.where(named_mask, route_weights[:, :, None].astype(jnp.float32), 0.0), axis=1
    )
    grouped = hit_table.reshape(total_rows // TOK_DEV, TOK_DEV, experts)
    rank_table = (jnp.cumsum(grouped, axis=1) - grouped).reshape(total_rows, experts)
    share_index = (jnp.arange(total_rows, dtype=jnp.int32) // TOK_DEV)[:, None]
    position_table = share_index * most_rows + rank_table
    return (hit_table, weight_table, rank_table, position_table)


def pick_slot(table, expert_count, slot_count, slot_index):
    shaped = table.reshape(table.shape[0], expert_count, slot_count)
    return lax.dynamic_index_in_dim(shaped, slot_index, 2, keepdims=False)


def shards(
    queries,
    keys_values,
    prefix_len,
    out_proj,
    residual,
    norm_gain,
    expert_ids,
    route_weights,
    w_gate,
    w_up,
    w_down,
):
    tensor_count = lax.axis_size("tensor")
    expert_count = lax.axis_size("expert")
    tensor_index = lax.axis_index("tensor")
    step_rows = queries.shape[0]
    per_device = queries.shape[1] // HD
    group_size = HEADS // KVH
    kv_index = tensor_index * per_device // group_size
    cached = lax.dynamic_index_in_dim(keys_values[0], kv_index, 0, keepdims=False)
    key_rows = cached[:, :HD]
    value_rows = cached[:, HD:]
    context = cached.shape[0]
    query_rows = queries.reshape(step_rows, per_device, HD)
    scores = jnp.einsum(
        "nhd,cd->hnc", query_rows, key_rows, preferred_element_type=jnp.float32
    ) / math.sqrt(HD)
    columns = jnp.arange(context, dtype=jnp.int32)[None, :]
    positions = jnp.arange(step_rows, dtype=jnp.int32)[:, None]
    visible = ((columns < prefix_len[0]) | (columns >= PREFIX) & (columns - PREFIX <= positions))[
        None
    ]
    highest = jnp.max(jnp.where(visible, scores, -1e30), axis=-1, keepdims=True)
    weights = jnp.exp(jnp.where(visible, scores - highest, -1e30))
    summed = jnp.sum(weights, axis=-1)
    blended = jnp.einsum(
        "hnc,cd->nhd", weights.astype(jnp.bfloat16), value_rows, preferred_element_type=jnp.float32
    )
    attended = (
        (blended / jnp.transpose(summed)[:, :, None])
        .astype(jnp.bfloat16)
        .reshape(step_rows, per_device * HD)
    )
    head_part = jnp.dot(
        attended,
        lax.all_gather(out_proj, "expert", axis=1, tiled=True),
        preferred_element_type=jnp.float32,
    )
    slot_count = tensor_count // HSPLIT
    experts = expert_count * slot_count
    most_rows = min(TOK_DEV, max(2, TOK_DEV * TOPK // experts + 1))
    capacity = tensor_count * most_rows
    slot_index = tensor_index // HSPLIT
    start_row = tensor_index * TOK_DEV
    hit_table, weight_table, rank_table, position_table = route_tables(
        expert_ids, route_weights, experts, most_rows
    )
    hit_slot = pick_slot(hit_table, expert_count, slot_count, slot_index)
    weight_slot = pick_slot(weight_table, expert_count, slot_count, slot_index)
    position_slot = pick_slot(position_table, expert_count, slot_count, slot_index)
    slot_match = (hit_slot[:, :, None] == 1) & (
        position_slot[:, :, None] == jnp.arange(capacity, dtype=jnp.int32)[None, None, :]
    )
    head_sum = lax.psum(head_part.astype(jnp.bfloat16), "tensor").astype(jnp.float32)
    residual_full = lax.all_gather(residual, "tensor", axis=0, tiled=True)
    state_full = (residual_full.astype(jnp.float32) + head_sum).astype(jnp.bfloat16)
    hidden_state = lax.dynamic_slice_in_dim(state_full, start_row, TOK_DEV, 0)
    normed_full = norm_rows(state_full, norm_gain)
    source_rows = jnp.sum(
        jnp.where(slot_match, jnp.arange(step_rows, dtype=jnp.int32)[:, None, None], 0), axis=0
    )
    filled = jnp.any(slot_match, axis=0)
    outgoing = jnp.where(
        filled[:, :, None], jnp.take(normed_full, source_rows, axis=0), jnp.zeros((), jnp.bfloat16)
    )
    arrived_rows = lax.all_to_all(outgoing, "expert", split_axis=0, concat_axis=0, tiled=True)
    flat_rows = arrived_rows.reshape(-1, arrived_rows.shape[-1])
    gate_val = jnp.dot(flat_rows, w_gate[0], preferred_element_type=jnp.float32)
    up_val = jnp.dot(flat_rows, w_up[0], preferred_element_type=jnp.float32)
    inner = (jax.nn.silu(gate_val) * up_val).astype(jnp.bfloat16)
    result = jnp.dot(inner, w_down[0], preferred_element_type=jnp.float32).astype(jnp.bfloat16)
    computed = result.reshape(arrived_rows.shape)
    returned = lax.all_to_all(computed, "expert", split_axis=0, concat_axis=0, tiled=True)
    combine_weights = jnp.where(slot_match, weight_slot[:, :, None], 0.0).astype(jnp.bfloat16)
    expert_part = jnp.einsum(
        "njc,jcd->nd", combine_weights, returned, preferred_element_type=jnp.float32
    )
    expert_share = lax.psum_scatter(
        expert_part.astype(jnp.bfloat16), "tensor", scatter_dimension=0, tiled=True
    ).astype(jnp.float32)
    return (hidden_state.astype(jnp.float32) + expert_share).astype(jnp.bfloat16)


def solution(mesh):
    return jax.shard_map(
        shards,
        mesh=mesh,
        in_specs=(
            P("expert", "tensor"),
            P("expert", None, None, None),
            P("expert"),
            P("tensor", "expert"),
            P(("expert", "tensor"), None),
            P(),
            P("expert", None),
            P("expert", None),
            P(("expert", "tensor"), None, None),
            P(("expert", "tensor"), None, None),
            P(("expert", "tensor"), None, None),
        ),
        out_specs=P(("expert", "tensor"), None),
        check_vma=False,
    )
```

profile of v0, /device:TPU:2, one launch (start us, length us, event | category | flops | bytes accessed | tf_op | source)
XLA Modules:
  0.0 520.2 jit_solution(15658658182001831944)
XLA Ops:
  6.5 0.7 all-gather.5.cloned.1.call-update
  7.3 0.7 all-gather.3.cloned.1.call-update
  8.1 0.8 convert_reduce_fusion
  8.9 0.1 copy.36
  9.7 1.1 copy.38
  10.7 1.9 reduce_window_sum.14
  12.7 2.0 dynamic-slice_bitcast_fusion
  14.7 1.0 fusion.26
  15.7 5.1 fusion.62
  20.8 2.4 fusion.33
  23.2 51.8 %all-gather.5.cloned.1.call-done = bf16[512,4096]{1,0:T(8,128)(2,1)} async-done(((bf16[512,256]{1,0:T(8,128)(2,1)}), bf16[512,4096]{1,0:T(8,128)(2,1)}) %all-gather.5.cloned.1.call-update) | async-done | bytes 4194320 | tf_op jit(solution)/shard_map/all_gather | solution.py:87
  75.0 4.8 convolution_convert_fusion.1
  79.8 0.9 fusion.57
  80.8 0.4 select_reduce_fusion
  81.2 0.1 reshape.155
  81.2 0.4 fusion.37
  81.6 34.7 %all-gather.3.cloned.1.call-done = bf16[256,4096]{1,0:T(8,128)(2,1)} async-done(((bf16[16,4096]{1,0:T(8,128)(2,1)}), bf16[256,4096]{1,0:T(8,128)(2,1)}) %all-gather.3.cloned.1.call-update) | async-done | bytes 2097168 | tf_op jit(solution)/shard_map/all_gather | solution.py:106
  116.4 115.7 %all-reduce.2.cloned.1.call-done = bf16[256,4096]{1,0:T(8,128)(2,1)} async-done(((bf16[256,4096]{1,0:T(8,128)(2,1)}), bf16[256,4096]{1,0:T(8,128)(2,1)}) %all-reduce.2.cloned.1.call-update) | async-done | bytes 2097168 | tf_op jit(solution)/shard_map/psum | solution.py:105
  232.1 3.2 fusion.6
  235.3 1.3 copy-done.1
  236.6 2.0 fusion.8
  238.6 13.8 %gather_fusion = bf16[768,4096]{1,0:T(8,128)(2,1)} fusion(bf16[256,4096]{1,0:T(8,128)(2,1)} %fusion.8, s32[1024]{0:T(1024)S(1)} %pad_clamp_fusion), kind=kCustom, calls=%fused_computation | custom fusion | bytes 12585984 | tf_op jit(solution)/shard_map/jit(_take)/gather | solution.py:115
  252.4 3.9 select_select_fusion
  256.3 79.0 %all_to_all.10 = bf16[16,48,4096]{2,1,0:T(8,128)(2,1)S(1)} all-to-all(bf16[16,48,4096]{2,1,0:T(8,128)(2,1)S(1)} %select_select_fusion), channel_id=1, replica_groups=mesh['expert'=16,'tensor'=16] {'expert'}, dimensions={0} | all-to-all | bytes 12582912 | tf_op jit(solution)/shard_map/all_to_all | solution.py:117
  335.3 3.4 fusion.12
  338.7 3.5 fusion.22
  342.2 5.4 %convolution_convert_fusion = bf16[768,4096]{1,0:T(8,128)(2,1)} fusion(bf16[768,384]{1,0:T(8,128)(2,1)S(1)} %fusion.22, bf16[1,384,4096]{2,1,0:T(8,128)(2,1)S(1)} %copy-done), kind=kOutput, calls=%fused_computation.2 | convolution fusion | flops 2419064832 | bytes 10027008 | tf_op jit(solution)/shard_map/dot_general | solution.py:122
  347.6 6.0 %all-to-all-start.1 = ((bf16[16,48,4096]{2,1,0:T(8,128)(2,1)}), bf16[16,48,4096]{2,1,0:T(8,128)(2,1)}, u32[]{:S(2)}, u32[]{:S(2)}) async-start(bf16[16,48,4096]{2,1,0:T(8,128)(2,1)} %bitcast.108), calls=%async_computation.1 | async-start | bytes 12582912 | tf_op jit(solution)/shard_map/all_to_all | solution.py:124
  353.8 87.2 %all-to-all-done.1 = bf16[16,48,4096]{2,1,0:T(8,128)(2,1)} async-done(((bf16[16,48,4096]{2,1,0:T(8,128)(2,1)}), bf16[16,48,4096]{2,1,0:T(8,128)(2,1)}, u32[]{:S(2)}, u32[]{:S(2)}) %all-to-all-start.1) | async-done | bytes 6291488 | tf_op jit(solution)/shard_map/all_to_all | solution.py:124
  441.0 6.0 %fusion.3 = bf16[256,4096]{1,0:T(8,128)(2,1)} fusion(bf16[16,48,4096]{2,1,0:T(8,128)(2,1)} %all-to-all-done.1, bf16[256,16]{0,1:T(8,128)(2,1)S(1)} %bitcast.119, s32[256,16]{0,1:T(8,128)S(1)} %bitcast.113, pred[256,16]{0,1:T(8,128)(4,1)S(1)} %bitcast.118), kind=kOutput, calls=%fused_computation.11 | convolution fusion | flops 1612251136 | bytes 8417280 | tf_op jit(solution)/shard_map/njc,jcd->nd/dot_general | solution.py:126
  447.0 65.0 %reduce-scatter.2.cloned.1.call-done = bf16[16,4096]{1,0:T(8,128)(2,1)} async-done(((bf16[256,4096]{1,0:T(8,128)(2,1)}), bf16[16,4096]{1,0:T(8,128)(2,1)}) %reduce-scatter.2.cloned.1.call-update) | async-done | bytes 131088 | tf_op jit(solution)/shard_map/reduce_scatter | solution.py:129
  512.0 1.7 add_convert_fusion.1
  (36 shorter events, 0.4 us)
Async XLA Ops:
  6.5 335.7 %copy-start = (bf16[1,384,4096]{2,1,0:T(8,128)(2,1)S(1)}, bf16[1,384,4096]{2,1,0:T(8,128)(2,1)}, u32[]{:S(2)}) copy-start(bf16[1,384,4096]{2,1,0:T(8,128)(2,1)} %param.21) | copy-start | bytes 9437188
  6.5 68.5 %all-gather.5.cloned.1.call-start = ((), (), s32[]{:S(2)}) async-start(), calls=%async_computation.4 | async-start | bytes 4456448 | tf_op jit(solution)/shard_map/all_gather | solution.py:87
  7.3 109.1 %all-gather.3.cloned.1.call-start = ((), (), s32[]{:S(2)}) async-start(), calls=%async_computation.3 | async-start | bytes 2228224 | tf_op jit(solution)/shard_map/all_gather | solution.py:106
  8.0 224.1 %all-reduce.2.cloned.1.call-start = ((), (), s32[]{:S(2)}) async-start(), calls=%async_computation.5 | async-start | bytes 4194304 | tf_op jit(solution)/shard_map/psum | solution.py:105
  79.8 156.8 %copy-start.3 = (f32[4096]{0:T(1024)S(1)}, f32[4096]{0:T(1024)}, u32[]{:S(2)}) copy-start(f32[4096]{0:T(1024)} %param.16) | copy-start | bytes 49156
  235.2 1.4 copy-start.1
  256.3 79.0 %copy-start.5 = (bf16[1,4096,384]{2,1,0:T(8,128)(2,1)S(1)}, bf16[1,4096,384]{2,1,0:T(8,128)(2,1)}, u32[]{:S(2)}) copy-start(bf16[1,4096,384]{2,1,0:T(8,128)(2,1)} %param.19) | copy-start | bytes 9437188
  335.3 3.4 copy-start.6
  347.6 6.0 %copy-start.4 = (bf16[256,8]{0,1:T(8,128)(2,1)S(1)}, bf16[256,8]{0,1:T(8,128)(2,1)}, u32[]{:S(2)}) copy-start(bf16[256,8]{0,1:T(8,128)(2,1)} %param.18) | copy-start | bytes 12292
  347.6 6.0 %copy-start.2 = (s32[256,8]{0,1:T(8,128)S(1)}, s32[256,8]{0,1:T(8,128)}, u32[]{:S(2)}) copy-start(s32[256,8]{0,1:T(8,128)} %param.17) | copy-start | bytes 24580
  347.6 93.4 %all-to-all-start.1 = ((bf16[16,48,4096]{2,1,0:T(8,128)(2,1)}), bf16[16,48,4096]{2,1,0:T(8,128)(2,1)}, u32[]{:S(2)}, u32[]{:S(2)}) async-start(bf16[16,48,4096]{2,1,0:T(8,128)(2,1)} %bitcast.108), calls=%async_computation.1 | async-start | bytes 12582912 | tf_op jit(solution)/shard_map/all_to_all | solution.py:124
  353.6 158.4 %reduce-scatter.2.cloned.1.call-start = ((), (), s32[]{:S(2)}) async-start(), calls=%async_computation.6 | async-start | bytes 2228224 | tf_op jit(solution)/shard_map/reduce_scatter | solution.py:129
Sparse Core Ops, SparseCore 0:
  9.8 65.2 all-gather.4
  76.8 39.4 all-gather.2
  118.7 113.3 all-reduce.1
  447.2 64.7 reduce-scatter.1
where the time goes:
time: 521 us; the launch traced here: 520 us
  waiting for transfers between devices  356 us (68%)
  blocking collectives  79 us (15%)
  matrix products  30.6 us (6%)
  local copies, waits for them, and re-layouts  20.5 us (4%)
  other arithmetic  14.3 us (3%)
  between operations  14 us (3%)
  starting transfers between devices  6.07 us (1%)
    psum x1, waiting for transfers between devices, shards(): lax.psum(head_part.astype(jnp.bfloat16), 'tensor').astype(jnp.float32)  116 us
    all_to_all x1, waiting for transfers between devices, shards(): lax.all_to_all(computed, 'expert', split_axis=0, concat_axis=0, tiled=True)  87.2 us
    all_to_all x1, blocking collectives, shards(): lax.all_to_all(outgoing, 'expert', split_axis=0, concat_axis=0, tiled=True)  79 us
    reduce_scatter x1, waiting for transfers between devices, shards(): lax.psum_scatter(expert_part.astype(jnp.bfloat16), 'tensor', scatter_dime...  65 us
    all_gather x1, waiting for transfers between devices, shards(): lax.all_gather(out_proj, 'expert', axis=1, tiled=True)  51.8 us
    all_gather x1, waiting for transfers between devices, shards(): residual_full = lax.all_gather(residual, 'tensor', axis=0, tiled=True)  34.7 us
    gather x1, local copies, waits for them, and re-layouts, shards(): jnp.take(normed_full, source_rows, axis=0)  13.8 us
  transfers between devices with their start and end apart: 5, of which 5 were waited for; matrix products, arithmetic and copies ran while one was open for 4% of the time, Pallas kernels for 0%

commit v1 on v0

--- a/solution.py
+++ b/solution.py
@@ -1,3 +1,4 @@
+import functools
 import math
 import jax
 import jax.numpy as jnp
@@ -11,6 +12,13 @@
 HSPLIT = 4
 TOK_DEV = 16
 PREFIX = 1024
+
+
+def get_works_on_mesh(z_in, row_axis):
+    return jnp.sum(lax.all_gather(z_in, axis_name=row_axis), axis=0)
+
+
+save_column_in = functools.partial(get_works_on_mesh, row_axis="tensor")
 
 
 def norm_rows(hidden_state, norm_gain):
@@ -102,7 +110,7 @@
     slot_match = (hit_slot[:, :, None] == 1) & (
         position_slot[:, :, None] == jnp.arange(capacity, dtype=jnp.int32)[None, None, :]
     )
-    head_sum = lax.psum(head_part.astype(jnp.bfloat16), "tensor").astype(jnp.float32)
+    head_sum = save_column_in(head_part.astype(jnp.bfloat16)).astype(jnp.float32)
     residual_full = lax.all_gather(residual, "tensor", axis=0, tiled=True)
     state_full = (residual_full.astype(jnp.float32) + head_sum).astype(jnp.bfloat16)
     hidden_state = lax.dynamic_slice_in_dim(state_full, start_row, TOK_DEV, 0)

time: 521 us -> 579 us (1.11)
  waiting for transfers between devices: 356 us -> 402 us
  other arithmetic: 14.3 us -> 25.7 us
    all_gather x0 -> x1, waiting for transfers between devices: none -> 170 us  [get_works_on_mesh(): return jnp.sum(lax.all_gather(z_in, axis_name=row_axis), axis=0)]
    psum x1 -> x0, waiting for transfers between devices: 116 us -> none  [shards(): lax.psum(head_part.astype(jnp.bfloat16), 'tensor').astype(jnp.float32)]
    reduce_sum x0 -> x1, other arithmetic: none -> 13 us  [get_works_on_mesh(): return jnp.sum(lax.all_gather(z_in, axis_name=row_axis), axis=0)]
    all_gather x1, waiting for transfers between devices: 34.7 us -> 27.2 us  [shards(): residual_full = lax.all_gather(residual, 'tensor', axis=0, tiled=True)]
  transfers between devices with their start and end apart: 5 -> 5, of which waited for: 5 -> 5; matrix products, arithmetic and copies ran while one was open for 4% -> 5% of each run, Pallas kernels for 0% -> 0%
where the time goes in v1:
time: 579 us
  waiting for transfers between devices  402 us (69%)
  blocking collectives  79.7 us (14%)
  matrix products  30.6 us (5%)
  other arithmetic  25.7 us (4%)
  local copies, waits for them, and re-layouts  19.8 us (3%)
  between operations  14.2 us (2%)
  starting transfers between devices  6.25 us (1%)
    all_gather x1, waiting for transfers between devices, get_works_on_mesh(): return jnp.sum(lax.all_gather(z_in, axis_name=row_axis), axis=0)  170 us
    all_to_all x1, waiting for transfers between devices, shards(): lax.all_to_all(computed, 'expert', split_axis=0, concat_axis=0, tiled=True)  88.4 us
    all_to_all x1, blocking collectives, shards(): lax.all_to_all(outgoing, 'expert', split_axis=0, concat_axis=0, tiled=True)  79.7 us
    reduce_scatter x1, waiting for transfers between devices, shards(): lax.psum_scatter(expert_part.astype(jnp.bfloat16), 'tensor', scatter_dime...  59.2 us
    all_gather x1, waiting for transfers between devices, shards(): lax.all_gather(out_proj, 'expert', axis=1, tiled=True)  56.4 us
    all_gather x1, waiting for transfers between devices, shards(): residual_full = lax.all_gather(residual, 'tensor', axis=0, tiled=True)  27.2 us
    gather x1, local copies, waits for them, and re-layouts, shards(): jnp.take(normed_full, source_rows, axis=0)  13.8 us
    reduce_sum x1, other arithmetic, get_works_on_mesh(): return jnp.sum(lax.all_gather(z_in, axis_name=row_axis), axis=0)  13 us
  transfers between devices with their start and end apart: 5, of which 5 were waited for; matrix products, arithmetic and copies ran while one was open for 5% of the time, Pallas kernels for 0%

profile of v1, /device:TPU:2, one launch (start us, length us, event | category | flops | bytes accessed | tf_op | source)
XLA Modules:
  0.0 578.7 jit_solution(2232472187698977132)
XLA Ops:
  6.5 0.7 all-gather.7.cloned.1.call-update
  8.2 2.0 dynamic-slice_bitcast_fusion
  10.1 1.0 fusion.26
  11.2 5.1 fusion.62
  16.2 2.4 fusion.33
  18.6 56.4 %all-gather.7.cloned.1.call-done = bf16[512,4096]{1,0:T(8,128)(2,1)} async-done(((bf16[512,256]{1,0:T(8,128)(2,1)}), bf16[512,4096]{1,0:T(8,128)(2,1)}) %all-gather.7.cloned.1.call-update) | async-done | bytes 4194320 | tf_op jit(solution)/shard_map/all_gather | solution.py:95
  75.0 4.8 convolution_convert_fusion.1
  79.9 0.2 all-gather.5.cloned.1.call-start
  80.1 0.5 all-gather.5.cloned.1.call-update
  80.7 0.1 copy.36
  80.9 1.1 copy.38
  82.0 1.3 reduce_window_sum.14
  83.4 0.4 select_reduce_fusion
  83.8 0.1 reshape.155
  83.8 0.4 fusion.37
  84.2 170.0 %all-gather.9.cloned.1.call-done = bf16[4096,4096]{1,0:T(8,128)(2,1)} async-done(((bf16[256,4096]{1,0:T(8,128)(2,1)}), bf16[4096,4096]{1,0:T(8,128)(2,1)}) %all-gather.9.cloned.1.call-update) | async-done | bytes 33554448 | tf_op jit(solution)/shard_map/all_gather | solution.py:18
  254.2 13.0 %reduce_sum.60 = bf16[256,4096]{1,0:T(8,128)(2,1)} reduce(bf16[16,256,4096]{2,1,0:T(8,128)(2,1)} %bitcast.108, bf16[]{:T(256)} %constant.95.clone.1), dimensions={0}, to_apply=%region_2.3 | reduce | flops 15728640 | bytes 35651584 | tf_op jit(solution)/shard_map/reduce_sum | solution.py:18
  267.2 27.2 %all-gather.5.cloned.1.call-done = bf16[256,4096]{1,0:T(8,128)(2,1)} async-done(((bf16[16,4096]{1,0:T(8,128)(2,1)}), bf16[256,4096]{1,0:T(8,128)(2,1)}) %all-gather.5.cloned.1.call-update) | async-done | bytes 2097168 | tf_op jit(solution)/shard_map/all_gather | solution.py:114
  294.4 3.2 fusion.6
  297.6 1.3 copy-done.1
  298.9 2.0 fusion.8
  300.9 13.8 %gather_fusion = bf16[768,4096]{1,0:T(8,128)(2,1)} fusion(bf16[256,4096]{1,0:T(8,128)(2,1)} %fusion.8, s32[1024]{0:T(1024)S(1)} %pad_clamp_fusion), kind=kCustom, calls=%fused_computation | custom fusion | bytes 12585984 | tf_op jit(solution)/shard_map/jit(_take)/gather | solution.py:123
  314.7 3.9 select_select_fusion
  318.6 79.7 %all_to_all.10 = bf16[16,48,4096]{2,1,0:T(8,128)(2,1)S(1)} all-to-all(bf16[16,48,4096]{2,1,0:T(8,128)(2,1)S(1)} %select_select_fusion), channel_id=1, replica_groups=mesh['expert'=16,'tensor'=16] {'expert'}, dimensions={0} | all-to-all | bytes 12582912 | tf_op jit(solution)/shard_map/all_to_all | solution.py:125
  398.3 3.4 fusion.12
  401.8 3.5 fusion.22
  405.3 5.4 convolution_convert_fusion
  410.7 6.0 %all-to-all-start.1 = ((bf16[16,48,4096]{2,1,0:T(8,128)(2,1)}), bf16[16,48,4096]{2,1,0:T(8,128)(2,1)}, u32[]{:S(2)}, u32[]{:S(2)}) async-start(bf16[16,48,4096]{2,1,0:T(8,128)(2,1)} %bitcast.110), calls=%async_computation.1 | async-start | bytes 12582912 | tf_op jit(solution)/shard_map/all_to_all | solution.py:132
  416.8 88.4 %all-to-all-done.1 = bf16[16,48,4096]{2,1,0:T(8,128)(2,1)} async-done(((bf16[16,48,4096]{2,1,0:T(8,128)(2,1)}), bf16[16,48,4096]{2,1,0:T(8,128)(2,1)}, u32[]{:S(2)}, u32[]{:S(2)}) %all-to-all-start.1) | async-done | bytes 6291488 | tf_op jit(solution)/shard_map/all_to_all | solution.py:132
  505.3 6.0 %fusion.3 = bf16[256,4096]{1,0:T(8,128)(2,1)} fusion(bf16[16,48,4096]{2,1,0:T(8,128)(2,1)} %all-to-all-done.1, bf16[256,16]{0,1:T(8,128)(2,1)S(1)} %bitcast.121, s32[256,16]{0,1:T(8,128)S(1)} %bitcast.115, pred[256,16]{0,1:T(8,128)(4,1)S(1)} %bitcast.120), kind=kOutput, calls=%fused_computation.11 | convolution fusion | flops 1612251136 | bytes 8417280 | tf_op jit(solution)/shard_map/njc,jcd->nd/dot_general | solution.py:134
  511.3 59.2 %reduce-scatter.2.cloned.1.call-done = bf16[16,4096]{1,0:T(8,128)(2,1)} async-done(((bf16[256,4096]{1,0:T(8,128)(2,1)}), bf16[16,4096]{1,0:T(8,128)(2,1)}) %reduce-scatter.2.cloned.1.call-update) | async-done | bytes 131088 | tf_op jit(solution)/shard_map/reduce_scatter | solution.py:137
  570.5 1.7 add_convert_fusion.1
  (37 shorter events, 0.5 us)
Async XLA Ops:
  6.5 398.7 %copy-start = (bf16[1,384,4096]{2,1,0:T(8,128)(2,1)S(1)}, bf16[1,384,4096]{2,1,0:T(8,128)(2,1)}, u32[]{:S(2)}) copy-start(bf16[1,384,4096]{2,1,0:T(8,128)(2,1)} %param.21) | copy-start | bytes 9437188
  6.5 68.5 %all-gather.7.cloned.1.call-start = ((), (), s32[]{:S(2)}) async-start(), calls=%async_computation.4 | async-start | bytes 4456448 | tf_op jit(solution)/shard_map/all_gather | solution.py:95
  7.3 246.9 %all-gather.9.cloned.1.call-start = ((), (), s32[]{:S(2)}) async-start(), calls=%async_computation.6 | async-start | bytes 35651584 | tf_op jit(solution)/shard_map/all_gather | solution.py:18
  75.0 5.6 copy-start.2
  79.9 214.5 %all-gather.5.cloned.1.call-start = ((), (), s32[]{:S(2)}) async-start(), calls=%async_computation.3 | async-start | bytes 2228224 | tf_op jit(solution)/shard_map/all_gather | solution.py:114
  267.2 31.7 %copy-start.3 = (f32[4096]{0:T(1024)S(1)}, f32[4096]{0:T(1024)}, u32[]{:S(2)}) copy-start(f32[4096]{0:T(1024)} %param.16) | copy-start | bytes 49156
  297.5 1.4 copy-start.1
  318.6 79.7 %copy-start.5 = (bf16[1,4096,384]{2,1,0:T(8,128)(2,1)S(1)}, bf16[1,4096,384]{2,1,0:T(8,128)(2,1)}, u32[]{:S(2)}) copy-start(bf16[1,4096,384]{2,1,0:T(8,128)(2,1)} %param.19) | copy-start | bytes 9437188
  398.3 3.4 copy-start.6
  410.7 6.0 %copy-start.4 = (bf16[256,8]{0,1:T(8,128)(2,1)S(1)}, bf16[256,8]{0,1:T(8,128)(2,1)}, u32[]{:S(2)}) copy-start(bf16[256,8]{0,1:T(8,128)(2,1)} %param.18) | copy-start | bytes 12292
  410.7 94.6 %all-to-all-start.1 = ((bf16[16,48,4096]{2,1,0:T(8,128)(2,1)}), bf16[16,48,4096]{2,1,0:T(8,128)(2,1)}, u32[]{:S(2)}, u32[]{:S(2)}) async-start(bf16[16,48,4096]{2,1,0:T(8,128)(2,1)} %bitcast.110), calls=%async_computation.1 | async-start | bytes 12582912 | tf_op jit(solution)/shard_map/all_to_all | solution.py:132
  416.6 153.9 %reduce-scatter.2.cloned.1.call-start = ((), (), s32[]{:S(2)}) async-start(), calls=%async_computation.5 | async-start | bytes 2228224 | tf_op jit(solution)/shard_map/reduce_scatter | solution.py:137
Sparse Core Ops, SparseCore 0:
  9.8 65.2 all-gather.6
  80.0 174.1 all-gather.8
  256.0 38.3 all-gather.4
  511.4 59.0 reduce-scatter.1
